TPU v7x, 32 devices: a whole 2x2x4 slice. The times are simulated.
32 devices in a mesh: row: 16 (over z, y, core), col: 2 (over x).
Axes of the slice: x: 2, y: 2, z: 4, core: 2. Of those that a mesh axis runs over, the one named last changes fastest.
Arguments:
- views: bfloat16 [81, 1024, 512], P(None, 'row', 'col'), may hold values from -6 to 6
Outputs:
- increment: float32 [1024, 512], P('row', 'col')
- residual: float32 [1024, 512], P('row', 'col')
All inputs are finite; a program needn't handle non-finite values.
Results may differ from a plain program's by a relative error of at most 0.0005.
Values may be sent and summed in bfloat16 or wider, within the bound.
A program may use at most 64 MiB of HBM per device.

v0:
```python
import functools

import jax
import jax.numpy as jnp
from jax import lax
from jax.experimental import pallas as pl
from jax.experimental.pallas import tpu as pltpu
from jax.sharding import PartitionSpec as P

ANG = 9
VIEWS = 81
HALF = 4
CENTER = 40
D0 = 3
smooth_weight = 2.0
damping = 0.1
PAD = 16
LANES = 128
F32 = jnp.float32
DIRS = ((-1, 0), (1, 0), (0, -1), (0, 1), (-1, -1), (-1, 1), (1, -1), (1, 1))


def roll(x, shift):
    return pltpu.roll(x, shift % LANES, 1)


def lane_of(rows):
    return lax.broadcasted_iota(jnp.int32, (rows, LANES), 1)


def kernel(nrow, ncol, views, out, ext, sp, col_r, col_l, fb, sb, band, pb, cen, cpack, acc, pacc, own, zc, gpack,
           ghost_u, ghost_d, ghost_l, ghost_r, corner, redbuf, redout, load_sem, send1, recv1, send2, recv2, rsend, rrecv, known):
    rows, cols = views.shape[1], views.shape[2]
    r, c = lax.axis_index("row"), lax.axis_index("col")
    count = nrow * ncol
    me = r * ncol + c
    full = PAD + rows + PAD

    def exists(dr, dc):
        return (r + dr >= 0) & (r + dr < nrow) & (c + dc >= 0) & (c + dc < ncol)

    barrier = pltpu.get_barrier_semaphore()

    def greet(sem, far):
        for dr, dc in DIRS:
            if abs(dr) * far < nrow and abs(dc) * far < ncol:
                @pl.when(exists(dr * far, dc * far))
                def _():
                    pl.semaphore_signal(sem, inc=1, device_id=(r + dr * far, c + dc * far), device_id_type=pl.DeviceIdType.MESH)

    def met(sem, far):
        total = 0
        for dr, dc in DIRS:
            if abs(dr) * far < nrow and abs(dc) * far < ncol:
                total = total + jnp.where(exists(dr * far, dc * far), 1, 0)
        pl.semaphore_wait(sem, total)

    greet(barrier, 1)
    reaches = []
    while 1 << len(reaches) < max(nrow, ncol) - 1:
        reaches.append(1 << len(reaches))

    def learn(step):
        if 0 < step <= len(reaches):
            met(known.at[step - 1], reaches[step - 1])
        if step < len(reaches):
            greet(known.at[step], reaches[step])

    loads = []
    for si in range(ANG):
        part = pl.ds(si * ANG, ANG)
        copy = pltpu.make_async_copy(views.at[part], ext.at[part, pl.ds(PAD, rows), :], load_sem.at[si])
        copy.start()
        loads.append(copy)

    def zero(ref, first, number, row, size):
        def body(i, carry):
            ref[first + i, row : row + size, :] = jnp.zeros((size, ref.shape[2]), ref.dtype)
            return carry
        lax.fori_loop(0, number, body, 0)

    @pl.when(r == 0)
    def _():
        zero(ext, 0, 41, 0, PAD)

    @pl.when(r == nrow - 1)
    def _():
        zero(ext, 40, 41, PAD + rows, PAD)

    for ref, edge in ((col_r, c == ncol - 1), (col_l, c == 0)):
        @pl.when(edge)
        def _():
            zero(ref, 0, 5, PAD, rows)

        @pl.when(edge | (r == 0))
        def _():
            zero(ref, 0, 3, 0, PAD)

        @pl.when(edge | (r == nrow - 1))
        def _():
            zero(ref, 2, 3, PAD + rows, PAD)

    for edge, ref in ((r == 0, ghost_u), (r == nrow - 1, ghost_d)):
        @pl.when(edge)
        def _():
            ref[0] = jnp.zeros((8, cols), F32)
            ref[1] = jnp.ones((8, cols), F32)
    for edge, ref, low in ((c == 0, ghost_l, 1.0), (c == ncol - 1, ghost_r, 0.0)):
        @pl.when(edge)
        def _():
            ref[...] = jnp.where(lane_of(rows) < 64, low, 1.0 - low)
    for index, (dr, dc) in enumerate(DIRS[4:]):
        @pl.when(jnp.logical_not(exists(-dr, -dc)))
        def _():
            corner[index] = jnp.zeros((8, LANES), F32)


    row_copies = []
    for size in range(HALF + 1):
        reach = 8 if D0 * size + 1 <= 8 else PAD
        for index, (dr, dc) in enumerate(DIRS[:2]):
            if size == 0:
                part = pl.ds(CENTER, 1)
            else:
                part = pl.ds(ANG * (HALF - dr * size), ANG)
            if dr < 0:
                src, dst = views.at[part, pl.ds(0, reach), :], ext.at[part, pl.ds(PAD + rows, reach), :]
            else:
                src, dst = views.at[part, pl.ds(rows - reach, reach), :], ext.at[part, pl.ds(PAD - reach, reach), :]
            row_copies.append((dr, dc, pltpu.make_async_remote_copy(
                src_ref=src, dst_ref=dst, send_sem=send1.at[2 * size + index], recv_sem=recv1.at[2 * size + index],
                device_id=(r + dr, c + dc), device_id_type=pl.DeviceIdType.MESH)))
    col_copies = []
    for index, (dr, dc) in enumerate(DIRS[2:]):
        side = col_r if dc < 0 else col_l
        mine = sp.at[0 if dc < 0 else 1]
        if dr == 0:
            src, dst = mine, side.at[:, pl.ds(PAD, rows), :]
        elif dr < 0:
            src, dst = mine.at[pl.ds(2, 3), pl.ds(0, PAD), :], side.at[pl.ds(2, 3), pl.ds(PAD + rows, PAD), :]
        else:
            src, dst = mine.at[pl.ds(0, 3), pl.ds(rows - PAD, PAD), :], side.at[pl.ds(0, 3), pl.ds(0, PAD), :]
        col_copies.append((dr, dc, pltpu.make_async_remote_copy(
            src_ref=src, dst_ref=dst, send_sem=send1.at[10 + index], recv_sem=recv1.at[10 + index],
            device_id=(r + dr, c + dc), device_id_type=pl.DeviceIdType.MESH)))

    def start(group):
        for dr, dc, copy in group:
            @pl.when(exists(dr, dc))
            def _():
                copy.start()

    def arrive(group):
        for dr, dc, copy in group:
            @pl.when(exists(-dr, -dc))
            def _():
                copy.wait_recv()

    def drain(group):
        for dr, dc, copy in group:
            @pl.when(exists(dr, dc))
            def _():
                copy.wait_send()

    offset = lax.broadcasted_iota(jnp.int32, (cols, cols), 0) - lax.broadcasted_iota(jnp.int32, (cols, cols), 1)
    plain = jnp.where(offset == 1, 1.0, jnp.where(offset == -1, -1.0, 0.0))
    for ti in range(ANG):
        band[ti] = (plain * float(ti - HALF)).astype(band.dtype)

    met(barrier, 1)
    start(row_copies)
    learn(0)
    for copy in loads:
        copy.wait()

    lane = lane_of(rows)
    group = (lane % 64) // 16
    place = lane % 16
    right_part = lane < 64

    for slot in range(5):
        left = right = None
        for half in range(2):
            if slot == 2 and half == 1:
                a = roll(ext[CENTER, PAD : PAD + rows, 0:LANES].astype(F32), 64)
                b = ext[CENTER, PAD : PAD + rows, cols - LANES : cols].astype(F32)
            else:
                si = (0, 2, 4, 5, 7)[slot] + half
                a = b = None
                for g in range(HALF):
                    x = ext[si * ANG + HALF + g + 1, PAD : PAD + rows, 0:LANES].astype(F32)
                    x = roll(x, 16 * g + 2 + 64 * half)
                    a = x if a is None else jnp.where(group == g, x, a)
                    x = ext[si * ANG + HALF - g - 1, PAD : PAD + rows, cols - LANES : cols].astype(F32)
                    x = roll(x, 16 * g + 14 + 64 * half)
                    b = x if b is None else jnp.where(group == g, x, b)
            left = a if half == 0 else jnp.where(right_part, left, a)
            right = b if half == 0 else jnp.where(right_part, right, b)
        sp[0, slot] = left.astype(sp.dtype)
        sp[1, slot] = right.astype(sp.dtype)
    start(col_copies)

    center = [ext[CENTER, PAD : PAD + rows, h * LANES : (h + 1) * LANES].astype(F32) for h in range(2)]
    ca, cb = center
    for ti in range(ANG):
        move = D0 * (ti - HALF)
        ra, rb = roll(ca, move), roll(cb, move)
        if move > 0:
            cen[ti, 0] = ra
            cen[ti, 1] = jnp.where(lane >= move, rb, ra)
        elif move < 0:
            cen[ti, 0] = jnp.where(lane < LANES + move, ra, rb)
            cen[ti, 1] = rb
        else:
            cen[ti, 0] = ca
            cen[ti, 1] = cb
    total = jnp.zeros((rows, LANES), F32)
    for g in range(HALF):
        m = D0 * (g + 1)
        total = jnp.where(right_part & (group == g), roll(cb, 16 * g - 126 + m), total)
        total = jnp.where((~right_part) & (group == g), roll(ca, 78 + 16 * g - m), total)
    cpack[...] = total
    pacc[...] = jnp.zeros_like(pacc)

    chunk = 16
    clane = lane_of(chunk)

    def terms(v0, side, down, s, middle):
        if s == 0:
            slope = side
        else:
            slope = side + (down if abs(s) == 1 else float(abs(s)) * down)
        error = v0 - middle
        weighted = slope * lax.rsqrt(1.0 + error * error)
        return weighted * slope, weighted * error

    def difference(ref, head, base, s):
        after, before = (base + 1, base - 1) if s > 0 else (base - 1, base + 1)
        return ref[head + (slice(after, after + chunk), slice(None))] - ref[head + (slice(before, before + chunk), slice(None))]

    def view_step(slot, s, at, middle, sums):
        base = PAD + D0 * s + at
        for h in range(2):
            v0, side = fb[slot, h, base : base + chunk, :], sb[slot, h, base : base + chunk, :]
            data, src = terms(v0, side, difference(fb, (slot, h), base, s) if s else None, s, middle[h])
            sums[0][h] = data if sums[0][h] is None else sums[0][h] + data
            sums[1][h] = src if sums[1][h] is None else sums[1][h] + src

    def widen(ti, slot, s, low, high):
        part = ext[ANG * (s + HALF) + ti, low:high, :]
        wide = part.astype(F32)
        side = jnp.dot(part, band[ti], preferred_element_type=F32)
        for h in range(2):
            fb[slot, h, low:high, :] = wide[:, h * LANES : (h + 1) * LANES]
            sb[slot, h, low:high, :] = side[:, h * LANES : (h + 1) * LANES]

    def needs_halo(s, at):
        return (s > 0 and at == rows - chunk) or (s < 0 and at == 0)

    def slot_of(ti, s):
        return (ti % 3) * ANG + s + HALF

    def inner_pass(ti):
        for s in range(-HALF, HALF + 1):
            widen(ti, slot_of(ti, s), s, PAD, PAD + rows)
        for at in range(0, rows, chunk):
            sums = [[None, None], [None, None]]
            middle = [cen[ti, h, at : at + chunk, :] for h in range(2)]
            for s in range(-HALF, HALF + 1):
                if not needs_halo(s, at):
                    view_step(slot_of(ti, s), s, at, middle, sums)
            for f in range(2):
                for h in range(2):
                    acc[ti, f, h, at : at + chunk, :] = sums[f][h]

    for ti in range(ANG):
        inner_pass(ti)
        if ti % 3 == 2:
            learn(ti // 3 + 1)
    arrive(row_copies[:2] + col_copies)
    frows, fcols = rows + 16, cols + 2 * LANES
    bands = []
    for part in (slice(0, PAD), slice(PAD, PAD + rows), slice(PAD + rows, full)):
        bands.append(jnp.concatenate([
            col_l[2, part, :].astype(F32), ext[CENTER, part, :].astype(F32), roll(col_r[2, part, :].astype(F32), 64)], axis=1))
    cf = jnp.concatenate([bands[0][8:16], bands[1], bands[2][0:8]], axis=0)
    gcol = lax.broadcasted_iota(jnp.int32, (frows, fcols), 1) + (c * cols - LANES)
    grow = lax.broadcasted_iota(jnp.int32, (frows, fcols), 0) + (r * rows - 8)

    def east(x):
        return pltpu.roll(x, fcols - 1, 1)

    def west(x):
        return pltpu.roll(x, 1, 1)

    def south(x):
        return pltpu.roll(x, frows - 1, 0)

    def north(x):
        return pltpu.roll(x, 1, 0)

    dx = east(cf) - cf
    dy = south(cf) - cf
    edge_e = jnp.where((gcol >= 0) & (gcol < ncol * cols - 1), smooth_weight * jnp.exp(-dx * dx), 0.0)
    edge_s = jnp.where((grow >= 0) & (grow < nrow * rows - 1), smooth_weight * jnp.exp(-dy * dy), 0.0)
    edge_w, edge_n = west(edge_e), north(edge_s)
    weights = edge_e + edge_w + edge_s + edge_n

    flane = lane_of(full)
    fgroup, fplace, fright = (flane % 64) // 16, flane % 16, flane < 64
    ptscale = jnp.where(clane < 64, 1.0, -1.0) * ((clane % 64) // 16 + 1).astype(F32)

    def packed_rows(si, low, high):
        slot, half = ((0, 0), (0, 1), (1, 0), (1, 1), (2, 0), (3, 0), (3, 1), (4, 0), (4, 1))[si]
        part = slice(low, high)
        right, grp, plc = fright[part], fgroup[part], fplace[part]
        x, z = col_r[slot, part, :].astype(F32), col_l[slot, part, :].astype(F32)
        merged = jnp.where(right, roll(x, 64) if half else x, z if half else roll(z, 64))
        for g in range(HALF):
            a = ext[si * ANG + HALF - g - 1, part, 0:LANES].astype(F32)
            b = ext[si * ANG + HALF + g + 1, part, cols - LANES : cols].astype(F32)
            merged = jnp.where(right & (grp == g) & (plc < 2), roll(b, 16 * g + 2), merged)
            merged = jnp.where((~right) & (grp == g) & (plc >= 14), roll(a, 16 * g + 78), merged)
        pb[si, part, :] = merged

    def packed_step(si, at):
        s = si - HALF
        base = PAD + D0 * s + at
        v0 = pb[si, base : base + chunk, :]
        side = ptscale * (roll(v0, -1) - roll(v0, 1))
        data, src = terms(v0, side, difference(pb, (si,), base, s) if s else None, s, cpack[at : at + chunk, :])
        pacc[0, at : at + chunk, :] += data
        pacc[1, at : at + chunk, :] += src

    def last_rows(si):
        return None if si == HALF else rows - chunk if si > HALF else 0

    for si in range(ANG):
        packed_rows(si, PAD, PAD + rows)
        for at in range(0, rows, chunk):
            if at != last_rows(si):
                packed_step(si, at)
    learn(4)

    def combine(low, high):
        part = slice(low, high)
        place_of = lane_of(high - low)
        for f in range(2):
            ta, tb = acc[HALF, f, 0, part, :], acc[HALF, f, 1, part, :]
            strip = pacc[f, part, :]
            for ti in range(ANG):
                m = D0 * abs(ti - HALF)
                if m == 0:
                    continue
                a, b = acc[ti, f, 0, part, :], acc[ti, f, 1, part, :]
                g = m // D0 - 1
                if ti > HALF:
                    ra, rb = roll(a, -m), roll(b, -m)
                    ta = ta + jnp.where(place_of < LANES - m, ra, rb)
                    tb = tb + jnp.where(place_of <= LANES - 2 - m, rb, roll(strip, 126 - m - 16 * g))
                else:
                    ra, rb = roll(a, m), roll(b, m)
                    ta = ta + jnp.where(place_of >= m + 1, ra, roll(strip, m - 78 - 16 * g))
                    tb = tb + jnp.where(place_of >= m, rb, ra)
            own[f, part, 0:LANES] = ta
            own[f, part, LANES : 2 * LANES] = tb

    def edge_size(size):
        for ti in range(ANG):
            for sign, at in ((1, rows - chunk), (-1, 0)):
                slot = 2 * ti + (sign < 0)
                low = PAD + at if sign > 0 else 0
                widen(ti, slot, sign * size, low, low + 2 * PAD)
            for sign, at in ((1, rows - chunk), (-1, 0)):
                slot = 2 * ti + (sign < 0)
                sums = [[acc[ti, f, h, at : at + chunk, :] for h in range(2)] for f in range(2)]
                middle = [cen[ti, h, at : at + chunk, :] for h in range(2)]
                view_step(slot, sign * size, at, middle, sums)
                for f in range(2):
                    for h in range(2):
                        acc[ti, f, h, at : at + chunk, :] = sums[f][h]
        for si in (HALF - size, HALF + size):
            low = PAD + rows if si > HALF else 0
            packed_rows(si, low, low + PAD)
            packed_step(si, last_rows(si))

    combine(chunk, rows - chunk)
    for size in range(1, HALF + 1):
        arrive(row_copies[2 * size : 2 * size + 2])
        edge_size(size)
    combine(0, chunk)
    combine(rows - chunk, rows)

    coeff = damping + own[0] * (0.25 / VIEWS)
    source = own[1] * (-0.5 / VIEWS)

    inner = (slice(8, 8 + rows), slice(LANES, LANES + cols))
    zed = source / (coeff + weights[inner])
    zc[0] = zed
    zc[1] = coeff
    gpack[0] = jnp.where(right_part, zed[:, 0:LANES], roll(coeff[:, 0:LANES], 64))
    gpack[1] = jnp.where(right_part, roll(coeff[:, cols - LANES : cols], 64), zed[:, cols - LANES : cols])

    copies2 = []
    for index, (dr, dc) in enumerate(DIRS):
        if dc == 0:
            src = zc.at[:, pl.ds(0, 8), :] if dr < 0 else zc.at[:, pl.ds(rows - 8, 8), :]
            dst = ghost_d if dr < 0 else ghost_u
        elif dr == 0:
            src = gpack.at[0] if dc < 0 else gpack.at[1]
            dst = ghost_r if dc < 0 else ghost_l
        else:
            src = gpack.at[0 if dc < 0 else 1, pl.ds(0 if dr < 0 else rows - 8, 8), :]
            dst = corner.at[index - 4]
        copies2.append((dr, dc, pltpu.make_async_remote_copy(
            src_ref=src, dst_ref=dst, send_sem=send2.at[index], recv_sem=recv2.at[index],
            device_id=(r + dr, c + dc), device_id_type=pl.DeviceIdType.MESH)))
    start(copies2)
    drain(row_copies + col_copies)
    for step in range(5, len(reaches) + 1):
        learn(step)
    arrive(copies2)

    zf = jnp.concatenate([
        jnp.concatenate([corner[3], ghost_u[0], corner[2]], axis=1),
        jnp.concatenate([ghost_l[...], zed, ghost_r[...]], axis=1),
        jnp.concatenate([corner[1], ghost_d[0], corner[0]], axis=1)], axis=0)
    one = jnp.ones((8, LANES), F32)
    kf = jnp.concatenate([
        jnp.concatenate([one, ghost_u[1], one], axis=1),
        jnp.concatenate([roll(ghost_l[...], 64), coeff, roll(ghost_r[...], 64)], axis=1),
        jnp.concatenate([one, ghost_d[1], one], axis=1)], axis=0)
    diag = kf + weights

    def gather(z):
        return edge_e * east(z) + edge_w * west(z) + edge_s * south(z) + edge_n * north(z)

    around = gather(zf)
    yf = around / diag
    n1, y = around[inner], yf[inner]
    n2 = gather(yf)[inner]
    w = source - n1
    q = zed - y
    wv = n1 - n2
    v = w - wv
    sums = (y * n1, q * n1, q * w, y * wv, y * v, q * v)
    line = lax.broadcasted_iota(jnp.int32, (1, LANES), 1)
    packed = jnp.zeros((1, LANES), F32)
    for i, x in enumerate(sums):
        x = jnp.sum(x, axis=0, keepdims=True)
        x = jnp.sum(x, axis=1, keepdims=True)
        packed = jnp.where(line == i, x, packed)
    redout[0] = packed
    redbuf[me] = packed

    def red_copy(i):
        peer = (me + i) % count
        return pltpu.make_async_remote_copy(
            src_ref=redout.at[0], dst_ref=redbuf.at[me], send_sem=rsend.at[0], recv_sem=rrecv.at[0],
            device_id=(peer // ncol, peer % ncol), device_id_type=pl.DeviceIdType.MESH)

    def cast_out(i, carry):
        red_copy(i).start()
        return carry

    lax.fori_loop(1, count, cast_out, 0)
    drain(copies2)
    others = redbuf.at[pl.ds(0, count - 1)]
    pltpu.make_async_copy(others, others, rrecv.at[0]).wait()
    pltpu.make_async_copy(others, others, rsend.at[0]).wait()
    totals = jnp.sum(redbuf[...], axis=0)
    f, g, h, k, l, m = [totals[:, i : i + 1] for i in range(6)]
    b, e = g + h, f + g
    delta = e / b
    step0 = (e + b) / b
    rz0 = e + b
    rz1 = f - 2.0 * delta * g + delta * delta * h
    wu1 = k - 2.0 * delta * l + delta * delta * m
    beta = rz1 / rz0
    step1 = rz1 / (wu1 - beta * rz1 / step0)
    direction = (y - delta * q) + beta * zed
    image = (wv - delta * v) + beta * w
    out[0] = step0 * zed + step1 * direction
    out[1] = (n1 - delta * w) - step1 * image


def solution(mesh):
    nrow, ncol = mesh.shape["row"], mesh.shape["col"]

    def shards(views):
        _, rows, cols = views.shape
        full = PAD + rows + PAD
        bf = views.dtype
        out = pl.pallas_call(
            functools.partial(kernel, nrow, ncol),
            out_shape=jax.ShapeDtypeStruct((2, rows, cols), F32),
            in_specs=[pl.BlockSpec(memory_space=pltpu.HBM)],
            out_specs=pl.BlockSpec(memory_space=pltpu.VMEM),
            scratch_shapes=[
                pltpu.VMEM((VIEWS, full, cols), bf),
                pltpu.VMEM((2, 5, rows, LANES), bf),
                pltpu.VMEM((5, full, LANES), bf),
                pltpu.VMEM((5, full, LANES), bf),
                pltpu.VMEM((3 * ANG, 2, full, LANES), F32),
                pltpu.VMEM((3 * ANG, 2, full, LANES), F32),
                pltpu.VMEM((ANG, cols, cols), bf),
                pltpu.VMEM((ANG, full, LANES), F32),
                pltpu.VMEM((ANG, 2, rows, LANES), F32),
                pltpu.VMEM((rows, LANES), F32),
                pltpu.VMEM((ANG, 2, 2, rows, LANES), F32),
                pltpu.VMEM((2, rows, LANES), F32),
                pltpu.VMEM((2, rows, cols), F32),
                pltpu.VMEM((2, rows, cols), F32),
                pltpu.VMEM((2, rows, LANES), F32),
                pltpu.VMEM((2, 8, cols), F32),
                pltpu.VMEM((2, 8, cols), F32),
                pltpu.VMEM((rows, LANES), F32),
                pltpu.VMEM((rows, LANES), F32),
                pltpu.VMEM((4, 8, LANES), F32),
                pltpu.VMEM((nrow * ncol, 1, LANES), F32),
                pltpu.VMEM((1, 1, LANES), F32),
                pltpu.SemaphoreType.DMA((ANG,)),
                pltpu.SemaphoreType.DMA((16,)),
                pltpu.SemaphoreType.DMA((16,)),
                pltpu.SemaphoreType.DMA((8,)),
                pltpu.SemaphoreType.DMA((8,)),
                pltpu.SemaphoreType.DMA((1,)),
                pltpu.SemaphoreType.DMA((1,)),
                pltpu.SemaphoreType.REGULAR((8,)),
            ],
            compiler_params=pltpu.CompilerParams(collective_id=0, has_side_effects=True, vmem_limit_bytes=48 << 20),
        )(pltpu.with_memory_space_constraint(views, pltpu.HBM))
        return out[0], out[1]

    return jax.shard_map(
        shards,
        mesh=mesh,
        in_specs=(P(None, "row", "col"),),
        out_specs=(P("row", "col"), P("row", "col")),
        check_vma=False,
    )
```

profile of v0, /device:TPU:0, one launch (start us, length us, event | category | flops | bytes accessed | tf_op | source)
XLA Modules:
  0.0 24.4 jit_solution(1550338983981599789)
XLA Ops:
  0.6 23.1 %shard_map.30 = f32[2,64,256]{2,1,0:T(8,128)S(1)} custom-call(bf16[81,64,256]{2,1,0:T(8,128)(2,1)} %views.1), custom_call_target="tpu_custom_call" | custom-call | tf_op jit(solution)/shard_map/pallas_call | solution.py:494
  23.8 0.7 %slice_bitcast_fusion = (f32[64,256]{1,0:T(8,128)}, f32[64,256]{1,0:T(8,128)}) fusion(f32[2,64,256]{2,1,0:T(8,128)S(1)} %shard_map.30), kind=kLoop, calls=%fused_computation | loop fusion | bytes 262144 | tf_op jit(solution)/shard_map/squeeze | solution.py:533
where the time goes:
time: 24.6 us; the launch traced here: 24.4 us
  Pallas kernels  23.1 us (94%)
  local copies, waits for them, and re-layouts  0.66 us (3%)
  between operations  0.64 us (3%)
    pallas_call x1, Pallas kernels, shards(): pl.pallas_call(functools.partial(kernel, nrow, ncol), out_shape=jax.Shape...  23.1 us
    squeeze x1, local copies, waits for them, and re-layouts, shards(): return (out[0], out[1])  0.66 us

commit v1 on v0

--- a/solution.py
+++ b/solution.py
@@ -15,6 +15,7 @@
 smooth_weight = 2.0
 damping = 0.1
 PAD = 16
+GROUPS = ((1, 2, 3), (4,))
 LANES = 128
 F32 = jnp.float32
 DIRS = ((-1, 0), (1, 0), (0, -1), (0, 1), (-1, -1), (-1, 1), (1, -1), (1, 1))
@@ -222,8 +223,7 @@
     cpack[...] = total
     pacc[...] = jnp.zeros_like(pacc)
 
-    chunk = 16
-    clane = lane_of(chunk)
+    chunk = 8
 
     def terms(v0, side, down, s, middle):
         if s == 0:
@@ -234,41 +234,47 @@
         weighted = slope * lax.rsqrt(1.0 + error * error)
         return weighted * slope, weighted * error
 
-    def difference(ref, head, base, s):
+    def difference(ref, head, base, size, s):
         after, before = (base + 1, base - 1) if s > 0 else (base - 1, base + 1)
-        return ref[head + (slice(after, after + chunk), slice(None))] - ref[head + (slice(before, before + chunk), slice(None))]
-
-    def view_step(slot, s, at, middle, sums):
+        return ref[head + (slice(after, after + size), slice(None))] - ref[head + (slice(before, before + size), slice(None))]
+
+    def view_step(k, s, at, middle, sums):
         base = PAD + D0 * s + at
         for h in range(2):
-            v0, side = fb[slot, h, base : base + chunk, :], sb[slot, h, base : base + chunk, :]
-            data, src = terms(v0, side, difference(fb, (slot, h), base, s) if s else None, s, middle[h])
+            v0, side = fb[k, h, base : base + chunk, :], sb[k, h, base : base + chunk, :]
+            data, src = terms(v0, side, difference(fb, (k, h), base, chunk, s) if s else None, s, middle[h])
             sums[0][h] = data if sums[0][h] is None else sums[0][h] + data
             sums[1][h] = src if sums[1][h] is None else sums[1][h] + src
 
-    def widen(ti, slot, s, low, high):
-        part = ext[ANG * (s + HALF) + ti, low:high, :]
+    def widen(ti, spans):
+        part = jnp.concatenate([ext[k, low:high, :] for k, low, high in spans], axis=0)
         wide = part.astype(F32)
         side = jnp.dot(part, band[ti], preferred_element_type=F32)
-        for h in range(2):
-            fb[slot, h, low:high, :] = wide[:, h * LANES : (h + 1) * LANES]
-            sb[slot, h, low:high, :] = side[:, h * LANES : (h + 1) * LANES]
-
-    def needs_halo(s, at):
-        return (s > 0 and at == rows - chunk) or (s < 0 and at == 0)
-
-    def slot_of(ti, s):
-        return (ti % 3) * ANG + s + HALF
+        first = 0
+        for k, low, high in spans:
+            rest = slice(first, first + high - low)
+            for h in range(2):
+                fb[k, h, low:high, :] = wide[rest, h * LANES : (h + 1) * LANES]
+                sb[k, h, low:high, :] = side[rest, h * LANES : (h + 1) * LANES]
+            first += high - low
+
+    def view_of(ti, s):
+        return ANG * (s + HALF) + ti
+
+    def inner_rows(s):
+        reach = -(-(D0 * abs(s) + 1) // chunk) * chunk if s else 0
+        return (reach if s < 0 else 0), (rows - reach if s > 0 else rows)
 
     def inner_pass(ti):
         for s in range(-HALF, HALF + 1):
-            widen(ti, slot_of(ti, s), s, PAD, PAD + rows)
+            widen(ti, [(view_of(ti, s), PAD, PAD + rows)])
         for at in range(0, rows, chunk):
             sums = [[None, None], [None, None]]
             middle = [cen[ti, h, at : at + chunk, :] for h in range(2)]
             for s in range(-HALF, HALF + 1):
-                if not needs_halo(s, at):
-                    view_step(slot_of(ti, s), s, at, middle, sums)
+                low, high = inner_rows(s)
+                if low <= at < high:
+                    view_step(view_of(ti, s), s, at, middle, sums)
             for f in range(2):
                 for h in range(2):
                     acc[ti, f, h, at : at + chunk, :] = sums[f][h]
@@ -308,7 +314,7 @@
 
     flane = lane_of(full)
     fgroup, fplace, fright = (flane % 64) // 16, flane % 16, flane < 64
-    ptscale = jnp.where(clane < 64, 1.0, -1.0) * ((clane % 64) // 16 + 1).astype(F32)
+    ptscale = jnp.where(lane < 64, 1.0, -1.0) * ((lane % 64) // 16 + 1).astype(F32)
 
     def packed_rows(si, low, high):
         slot, half = ((0, 0), (0, 1), (1, 0), (1, 1), (2, 0), (3, 0), (3, 1), (4, 0), (4, 1))[si]
@@ -323,23 +329,18 @@
             merged = jnp.where((~right) & (grp == g) & (plc >= 14), roll(a, 16 * g + 78), merged)
         pb[si, part, :] = merged
 
-    def packed_step(si, at):
+    def packed_step(si, low, high):
         s = si - HALF
-        base = PAD + D0 * s + at
-        v0 = pb[si, base : base + chunk, :]
-        side = ptscale * (roll(v0, -1) - roll(v0, 1))
-        data, src = terms(v0, side, difference(pb, (si,), base, s) if s else None, s, cpack[at : at + chunk, :])
-        pacc[0, at : at + chunk, :] += data
-        pacc[1, at : at + chunk, :] += src
-
-    def last_rows(si):
-        return None if si == HALF else rows - chunk if si > HALF else 0
+        base, size = PAD + D0 * s + low, high - low
+        v0 = pb[si, base : base + size, :]
+        side = ptscale[low:high] * (roll(v0, -1) - roll(v0, 1))
+        data, src = terms(v0, side, difference(pb, (si,), base, size, s) if s else None, s, cpack[low:high, :])
+        pacc[0, low:high, :] += data
+        pacc[1, low:high, :] += src
 
     for si in range(ANG):
         packed_rows(si, PAD, PAD + rows)
-        for at in range(0, rows, chunk):
-            if at != last_rows(si):
-                packed_step(si, at)
+        packed_step(si, *inner_rows(si - HALF))
     learn(4)
 
     def combine(low, high):
@@ -365,31 +366,38 @@
             own[f, part, 0:LANES] = ta
             own[f, part, LANES : 2 * LANES] = tb
 
-    def edge_size(size):
+    def edge_sizes(sizes):
         for ti in range(ANG):
-            for sign, at in ((1, rows - chunk), (-1, 0)):
-                slot = 2 * ti + (sign < 0)
-                low = PAD + at if sign > 0 else 0
-                widen(ti, slot, sign * size, low, low + 2 * PAD)
-            for sign, at in ((1, rows - chunk), (-1, 0)):
-                slot = 2 * ti + (sign < 0)
+            spans = []
+            for size in sizes:
+                spans.append((view_of(ti, size), PAD + rows, PAD + rows + PAD))
+                spans.append((view_of(ti, -size), 0, PAD))
+            widen(ti, spans)
+            for at in (0, chunk, rows - 2 * chunk, rows - chunk):
                 sums = [[acc[ti, f, h, at : at + chunk, :] for h in range(2)] for f in range(2)]
                 middle = [cen[ti, h, at : at + chunk, :] for h in range(2)]
-                view_step(slot, sign * size, at, middle, sums)
+                for size in sizes:
+                    s = -size if at < rows // 2 else size
+                    low, high = inner_rows(s)
+                    if not low <= at < high:
+                        view_step(view_of(ti, s), s, at, middle, sums)
                 for f in range(2):
                     for h in range(2):
                         acc[ti, f, h, at : at + chunk, :] = sums[f][h]
-        for si in (HALF - size, HALF + size):
-            low = PAD + rows if si > HALF else 0
-            packed_rows(si, low, low + PAD)
-            packed_step(si, last_rows(si))
-
-    combine(chunk, rows - chunk)
-    for size in range(1, HALF + 1):
-        arrive(row_copies[2 * size : 2 * size + 2])
-        edge_size(size)
-    combine(0, chunk)
-    combine(rows - chunk, rows)
+        for size in sizes:
+            for s in (-size, size):
+                first = 0 if s < 0 else PAD + rows
+                packed_rows(HALF + s, first, first + PAD)
+                low, high = inner_rows(s)
+                packed_step(HALF + s, *((0, low) if s < 0 else (high, rows)))
+
+    combine(PAD, rows - PAD)
+    for sizes in GROUPS:
+        for size in sizes:
+            arrive(row_copies[2 * size : 2 * size + 2])
+        edge_sizes(sizes)
+    combine(0, PAD)
+    combine(rows - PAD, rows)
 
     coeff = damping + own[0] * (0.25 / VIEWS)
     source = own[1] * (-0.5 / VIEWS)
@@ -501,8 +509,8 @@
                 pltpu.VMEM((2, 5, rows, LANES), bf),
                 pltpu.VMEM((5, full, LANES), bf),
                 pltpu.VMEM((5, full, LANES), bf),
-                pltpu.VMEM((3 * ANG, 2, full, LANES), F32),
-                pltpu.VMEM((3 * ANG, 2, full, LANES), F32),
+                pltpu.VMEM((VIEWS, 2, full, LANES), F32),
+                pltpu.VMEM((VIEWS, 2, full, LANES), F32),
                 pltpu.VMEM((ANG, cols, cols), bf),
                 pltpu.VMEM((ANG, full, LANES), F32),
                 pltpu.VMEM((ANG, 2, rows, LANES), F32),

time: 24.6 us -> 23.3 us (0.947)
  Pallas kernels: 23.1 us -> 21.9 us
    pallas_call x1, Pallas kernels: 23.1 us -> 21.9 us  [shards(): pl.pallas_call(functools.partial(kernel, nrow, ncol), out_shape=jax.Shape...]
where the time goes in v1:
time: 23.3 us; the launch traced here: 23.2 us
  Pallas kernels  21.9 us (94%)
  local copies, waits for them, and re-layouts  0.66 us (3%)
  between operations  0.64 us (3%)
    pallas_call x1, Pallas kernels, shards(): pl.pallas_call(functools.partial(kernel, nrow, ncol), out_shape=jax.Shape...  21.9 us
    squeeze x1, local copies, waits for them, and re-layouts, shards(): return (out[0], out[1])  0.66 us

profile of v1, /device:TPU:0, one launch (start us, length us, event | category | flops | bytes accessed | tf_op | source)
XLA Modules:
  0.0 23.2 jit_solution(1205769777760780187)
XLA Ops:
  0.6 21.9 %shard_map.30 = f32[2,64,256]{2,1,0:T(8,128)S(1)} custom-call(bf16[81,64,256]{2,1,0:T(8,128)(2,1)} %views.1), custom_call_target="tpu_custom_call" | custom-call | tf_op jit(solution)/shard_map/pallas_call | solution.py:502
  22.5 0.7 %slice_bitcast_fusion = (f32[64,256]{1,0:T(8,128)}, f32[64,256]{1,0:T(8,128)}) fusion(f32[2,64,256]{2,1,0:T(8,128)S(1)} %shard_map.30), kind=kLoop, calls=%fused_computation | loop fusion | bytes 262144 | tf_op jit(solution)/shard_map/squeeze | solution.py:541

commit v2 on v1

v2 whole, which is shorter than its diff:
```python
import functools

import jax
import jax.numpy as jnp
from jax import lax
from jax.experimental import pallas as pl
from jax.experimental.pallas import tpu as pltpu
from jax.sharding import PartitionSpec as P

ANG = 9
VIEWS = 81
HALF = 4
CENTER = 40
D0 = 3
smooth_weight = 2.0
damping = 0.1
PAD = 16
RING = 8
GROUPS = ((0, 1, 2, 3), (4,))
STRIP = (50, 42, 31, 17, 0)
LANES = 128
F32 = jnp.float32
DIRS = ((-1, 0), (1, 0), (0, -1), (0, 1), (-1, -1), (-1, 1), (1, -1), (1, 1))


def roll(x, shift):
    return pltpu.roll(x, shift % LANES, 1)


def lane_of(rows):
    return lax.broadcasted_iota(jnp.int32, (rows, LANES), 1)


def kernel(nrow, ncol, views, out, ext, sp, col_r, col_l, side_r, side_l, fb, sb, band, pb, cen, cpack, acc, pacc, own,
           redbuf, redout, load_sem, send1, recv1, rsend, rrecv, known):
    rows, cols = views.shape[1], views.shape[2]
    r, c = lax.axis_index("row"), lax.axis_index("col")
    count = nrow * ncol
    me = r * ncol + c
    full = PAD + rows + PAD

    def exists(dr, dc):
        return (r + dr >= 0) & (r + dr < nrow) & (c + dc >= 0) & (c + dc < ncol)

    barrier = pltpu.get_barrier_semaphore()

    def greet(sem, far, dirs):
        for dr, dc in dirs:
            if abs(dr) * far < nrow and abs(dc) * far < ncol:
                @pl.when(exists(dr * far, dc * far))
                def _():
                    pl.semaphore_signal(sem, inc=1, device_id=(r + dr * far, c + dc * far), device_id_type=pl.DeviceIdType.MESH)

    def met(sem, far, dirs):
        total = 0
        for dr, dc in dirs:
            if abs(dr) * far < nrow and abs(dc) * far < ncol:
                total = total + jnp.where(exists(dr * far, dc * far), 1, 0)
        pl.semaphore_wait(sem, total)

    greet(barrier, 1, DIRS[:4])
    rounds = [(1, DIRS[:4])]
    while len(rounds) == 1 or 2 * rounds[-1][0] < max(nrow, ncol) - 1:
        rounds.append((1 << (len(rounds) - 1), DIRS))

    def learn(step):
        if 0 < step <= len(rounds):
            met(known.at[step - 1], *rounds[step - 1])
        if step < len(rounds):
            greet(known.at[step], *rounds[step])

    loads = []
    for si in range(ANG):
        part = pl.ds(si * ANG, ANG)
        copy = pltpu.make_async_copy(views.at[part], ext.at[part, pl.ds(PAD, rows), :], load_sem.at[si])
        copy.start()
        loads.append(copy)

    def zero(ref, first, number, row, size):
        def body(i, carry):
            ref[first + i, row : row + size, :] = jnp.zeros((size, ref.shape[2]), ref.dtype)
            return carry
        lax.fori_loop(0, number, body, 0)

    @pl.when(r == 0)
    def _():
        zero(ext, 0, 41, 0, PAD)

    @pl.when(r == nrow - 1)
    def _():
        zero(ext, 40, 41, PAD + rows, PAD)

    for ref, edge in ((col_r, c == ncol - 1), (col_l, c == 0)):
        @pl.when(edge)
        def _():
            zero(ref, 0, 5, PAD, rows)

        @pl.when(edge | (r == 0))
        def _():
            zero(ref, 0, 3, 0, PAD)

        @pl.when(edge | (r == nrow - 1))
        def _():
            zero(ref, 2, 3, PAD + rows, PAD)

    row_copies = []
    for size in range(HALF + 1):
        reach = 8 if D0 * size + 3 <= 8 else PAD
        for index, (dr, dc) in enumerate(DIRS[:2]):
            if size == 0:
                part = pl.ds(ANG * HALF, ANG)
            else:
                part = pl.ds(ANG * (HALF - dr * size), ANG)
            if dr < 0:
                src, dst = views.at[part, pl.ds(0, reach), :], ext.at[part, pl.ds(PAD + rows, reach), :]
            else:
                src, dst = views.at[part, pl.ds(rows - reach, reach), :], ext.at[part, pl.ds(PAD - reach, reach), :]
            row_copies.append((dr, dc, pltpu.make_async_remote_copy(
                src_ref=src, dst_ref=dst, send_sem=send1.at[2 * size + index], recv_sem=recv1.at[2 * size + index],
                device_id=(r + dr, c + dc), device_id_type=pl.DeviceIdType.MESH)))
    col_copies = []
    for index, (dr, dc) in enumerate(DIRS[2:]):
        side = col_r if dc < 0 else col_l
        mine = sp.at[0 if dc < 0 else 1]
        if dr == 0:
            src, dst = mine, side.at[:, pl.ds(PAD, rows), :]
        elif dr < 0:
            src, dst = mine.at[pl.ds(2, 3), pl.ds(0, PAD), :], side.at[pl.ds(2, 3), pl.ds(PAD + rows, PAD), :]
        else:
            src, dst = mine.at[pl.ds(0, 3), pl.ds(rows - PAD, PAD), :], side.at[pl.ds(0, 3), pl.ds(0, PAD), :]
        col_copies.append((dr, dc, pltpu.make_async_remote_copy(
            src_ref=src, dst_ref=dst, send_sem=send1.at[10 + index], recv_sem=recv1.at[10 + index],
            device_id=(r + dr, c + dc), device_id_type=pl.DeviceIdType.MESH)))

    side_copies = []
    for index, (dr, dc) in enumerate(DIRS[2:]):
        side = side_r if dc < 0 else side_l
        tile = pl.ds(0 if dc < 0 else cols - LANES, LANES)
        first, number, into = ((0, rows, PAD), (rows - RING, RING, PAD - RING), (0, RING, PAD + rows))[dr]
        side_copies.append((dr, dc, pltpu.make_async_remote_copy(
            src_ref=views.at[CENTER, pl.ds(first, number), tile], dst_ref=side.at[pl.ds(into, number), :],
            send_sem=send1.at[16 + index], recv_sem=recv1.at[16 + index],
            device_id=(r + dr, c + dc), device_id_type=pl.DeviceIdType.MESH)))

    def start(group):
        for dr, dc, copy in group:
            @pl.when(exists(dr, dc))
            def _():
                copy.start()

    def arrive(group):
        for dr, dc, copy in group:
            @pl.when(exists(-dr, -dc))
            def _():
                copy.wait_recv()

    def drain(group):
        for dr, dc, copy in group:
            @pl.when(exists(dr, dc))
            def _():
                copy.wait_send()

    offset = lax.broadcasted_iota(jnp.int32, (cols, cols), 0) - lax.broadcasted_iota(jnp.int32, (cols, cols), 1)
    plain = jnp.where(offset == 1, 1.0, jnp.where(offset == -1, -1.0, 0.0))
    for ti in range(ANG):
        band[ti] = (plain * float(ti - HALF)).astype(band.dtype)

    met(barrier, 1, DIRS[:4])
    start(row_copies)
    start(side_copies[:2])
    learn(0)
    for copy in loads:
        copy.wait()

    lane = lane_of(rows)
    right_part = lane < 64

    def own_start(t):
        return STRIP[t] + (2 if t else 1)

    for slot, pair in enumerate(((0, 1), (2, 3), (4,), (5, 6), (7, 8))):
        left = right = None
        for half, si in enumerate(pair):
            for t in range(HALF, -1, -1):
                first = own_start(t) + 64 * half
                x = roll(ext[si * ANG + HALF + t, PAD : PAD + rows, 0:LANES].astype(F32), first)
                left = x if left is None else jnp.where(lane >= first, x, left)
        for half, si in reversed(list(enumerate(pair))):
            for t in range(HALF, -1, -1):
                first = STRIP[t] + 64 * (1 - half)
                x = roll(ext[si * ANG + HALF - t, PAD : PAD + rows, cols - LANES : cols].astype(F32), first - (LANES - 3 - D0 * t))
                right = x if right is None else jnp.where(lane >= first, x, right)
        sp[0, slot] = left.astype(sp.dtype)
        sp[1, slot] = right.astype(sp.dtype)
    start(col_copies[:2])
    learn(1)
    start(side_copies[2:] + col_copies[2:])
    arrive(side_copies[:2])

    def build_center(low, high):
        part, into = slice(PAD + low, PAD + high), slice(RING + low, RING + high)
        at = lane_of(high - low)
        tl, tr = side_l[part, :].astype(F32), side_r[part, :].astype(F32)
        ta, tb = [ext[CENTER, part, h * LANES : (h + 1) * LANES].astype(F32) for h in range(2)]
        for ti in range(ANG):
            move = D0 * (ti - HALF)
            if move > 0:
                ra = roll(ta, move)
                cen[ti, 0, into, :] = jnp.where(at >= move, ra, roll(tl, move))
                cen[ti, 1, into, :] = jnp.where(at >= move, roll(tb, move), ra)
            elif move < 0:
                rb = roll(tb, move)
                cen[ti, 0, into, :] = jnp.where(at < LANES + move, roll(ta, move), rb)
                cen[ti, 1, into, :] = jnp.where(at < LANES + move, rb, roll(tr, move))
            else:
                cen[ti, 0, into, :] = ta
                cen[ti, 1, into, :] = tb
        total = None
        for t in range(HALF, -1, -1):
            m = D0 * t
            first = STRIP[t]
            inside = own_start(t) + m
            x = jnp.where(at >= inside, roll(tr, inside), roll(tb, inside))
            total = x if total is None else jnp.where(at >= first, x, total)
        for t in range(HALF, -1, -1):
            first = 64 + STRIP[t]
            x = jnp.where(at >= first + 3, roll(ta, first + 3), roll(tl, first + 3))
            total = jnp.where(at >= first, x, total)
        cpack[into, :] = total

    build_center(0, rows)
    pacc[...] = jnp.zeros_like(pacc)

    chunk = 8

    def terms(v0, side, down, s, middle):
        if s == 0:
            slope = side
        else:
            slope = side + (down if abs(s) == 1 else float(abs(s)) * down)
        error = v0 - middle
        weighted = slope * lax.rsqrt(1.0 + error * error)
        return weighted * slope, weighted * error

    def difference(ref, head, base, size, s):
        after, before = (base + 1, base - 1) if s > 0 else (base - 1, base + 1)
        return ref[head + (slice(after, after + size), slice(None))] - ref[head + (slice(before, before + size), slice(None))]

    def view_step(k, s, at, middle, sums):
        base = RING + PAD + D0 * s + at
        for h in range(2):
            v0, side = fb[k, h, base : base + chunk, :], sb[k, h, base : base + chunk, :]
            data, src = terms(v0, side, difference(fb, (k, h), base, chunk, s) if s else None, s, middle[h])
            sums[0][h] = data if sums[0][h] is None else sums[0][h] + data
            sums[1][h] = src if sums[1][h] is None else sums[1][h] + src

    def widen(ti, spans):
        part = jnp.concatenate([ext[k, low:high, :] for k, low, high in spans], axis=0)
        wide = part.astype(F32)
        side = jnp.dot(part, band[ti], preferred_element_type=F32)
        first = 0
        for k, low, high in spans:
            rest = slice(first, first + high - low)
            for h in range(2):
                fb[k, h, RING + low : RING + high, :] = wide[rest, h * LANES : (h + 1) * LANES]
                sb[k, h, RING + low : RING + high, :] = side[rest, h * LANES : (h + 1) * LANES]
            first += high - low

    def view_of(ti, s):
        return ANG * (s + HALF) + ti

    def inner_rows(s):
        reach = -(-(D0 * abs(s) + 1) // chunk) * chunk if s else 0
        return (reach if s < 0 else 0), (rows - reach if s > 0 else rows)

    def inner_pass(ti):
        for s in range(-HALF, HALF + 1):
            widen(ti, [(view_of(ti, s), PAD, PAD + rows)])
        for at in range(0, rows, chunk):
            sums = [[None, None], [None, None]]
            middle = [cen[ti, h, RING + at : RING + at + chunk, :] for h in range(2)]
            for s in range(-HALF, HALF + 1):
                low, high = inner_rows(s)
                if low <= at < high:
                    view_step(view_of(ti, s), s, at, middle, sums)
            for f in range(2):
                for h in range(2):
                    acc[ti, f, h, RING + at : RING + at + chunk, :] = sums[f][h]

    for ti in range(ANG):
        inner_pass(ti)
        if ti % 3 == 2:
            learn(ti // 3 + 2)
    arrive(row_copies[:2] + col_copies + side_copies[2:])
    build_center(-RING, 0)
    build_center(rows, rows + RING)
    frows, fcols = rows + 16, cols + 2 * LANES
    middle_rows = slice(PAD - RING, PAD + rows + RING)
    cf = jnp.concatenate([
        side_l[0:full, :].astype(F32), ext[CENTER, 0:full, :].astype(F32), side_r[0:full, :].astype(F32)], axis=1)[middle_rows]
    gcol = lax.broadcasted_iota(jnp.int32, (frows, fcols), 1) + (c * cols - LANES)
    grow = lax.broadcasted_iota(jnp.int32, (frows, fcols), 0) + (r * rows - 8)

    def east(x):
        return pltpu.roll(x, fcols - 1, 1)

    def west(x):
        return pltpu.roll(x, 1, 1)

    def south(x):
        return pltpu.roll(x, frows - 1, 0)

    def north(x):
        return pltpu.roll(x, 1, 0)

    dx = east(cf) - cf
    dy = south(cf) - cf
    edge_e = jnp.where((gcol >= 0) & (gcol < ncol * cols - 1), smooth_weight * jnp.exp(-dx * dx), 0.0)
    edge_s = jnp.where((grow >= 0) & (grow < nrow * rows - 1), smooth_weight * jnp.exp(-dy * dy), 0.0)
    edge_w, edge_n = west(edge_e), north(edge_s)
    weights = edge_e + edge_w + edge_s + edge_n

    def packed_rows(si, low, high):
        slot, half = ((0, 0), (0, 1), (1, 0), (1, 1), (2, 0), (3, 0), (3, 1), (4, 0), (4, 1))[si]
        at = lane_of(high - low)
        part = slice(low, high)
        x, z = col_r[slot, part, :].astype(F32), col_l[slot, part, :].astype(F32)
        merged = roll(jnp.where(at < 64, z, x), 64) if half else jnp.where(at < 64, x, z)
        for t in range(HALF + 1):
            a = ext[si * ANG + HALF - t, part, 0:LANES].astype(F32)
            b = ext[si * ANG + HALF + t, part, cols - LANES : cols].astype(F32)
            first, last = STRIP[t], own_start(t) - 1
            own_b = (at >= first) & (at <= last) if t else at == first
            merged = jnp.where(own_b, roll(b, last - (LANES - 1)), merged)
            first = 64 + STRIP[t] + 3 + D0 * t
            own_a = (at == first) | (at == first + 1) if t else at == first
            merged = jnp.where(own_a, roll(a, first), merged)
        pb[si, RING + low : RING + high, :] = merged

    def packed_step(si, low, high):
        s = si - HALF
        base, size = RING + PAD + D0 * s + low, high - low
        at = lane_of(size)
        scale = jnp.zeros((size, LANES), F32)
        for t in range(1, HALF + 1):
            span = 5 + D0 * t
            scale = jnp.where((at >= STRIP[t]) & (at < STRIP[t] + span), float(t), scale)
            scale = jnp.where((at >= 64 + STRIP[t]) & (at < 64 + STRIP[t] + span), float(-t), scale)
        v0 = pb[si, base : base + size, :]
        side = scale * (roll(v0, -1) - roll(v0, 1))
        part = slice(RING + low, RING + high)
        data, src = terms(v0, side, difference(pb, (si,), base, size, s) if s else None, s, cpack[part, :])
        pacc[0, part, :] += data
        pacc[1, part, :] += src

    for si in range(ANG):
        packed_rows(si, PAD, PAD + rows)
        packed_step(si, *inner_rows(si - HALF))
    learn(5)

    def combine(low, high):
        part = slice(RING + low, RING + high)
        at = lane_of(high - low)
        for f in range(2):
            ta, tb = acc[HALF, f, 0, part, :], acc[HALF, f, 1, part, :]
            strip = pacc[f, part, :]
            el, er = roll(strip, 61 - STRIP[0]), roll(strip, -own_start(0))
            for ti in range(ANG):
                m = D0 * abs(ti - HALF)
                if m == 0:
                    continue
                a, b = acc[ti, f, 0, part, :], acc[ti, f, 1, part, :]
                t = m // D0
                if ti > HALF:
                    ra, rb, rs = roll(a, -m), roll(b, -m), roll(strip, 126 - m - STRIP[t])
                    ta = ta + jnp.where(at < LANES - m, ra, rb)
                    tb = tb + jnp.where(at <= LANES - 2 - m, rb, rs)
                    el, er = el + ra, er + rs
                else:
                    ra, rb, rs = roll(a, m), roll(b, m), roll(strip, -67 - STRIP[t])
                    ta = ta + jnp.where(at >= m + 1, ra, rs)
                    tb = tb + jnp.where(at >= m, rb, ra)
                    el, er = el + rs, er + rb
            for tile, total in enumerate((el, ta, tb, er)):
                own[f, part, tile * LANES : (tile + 1) * LANES] = total

    def edge_sizes(sizes):
        for ti in range(ANG):
            spans = []
            for size in sizes:
                spans.append((view_of(ti, size), PAD + rows, PAD + rows + PAD))
                spans.append((view_of(ti, -size), 0, PAD))
            widen(ti, spans)
            for at in (-RING, 0, chunk, rows - 2 * chunk, rows - chunk, rows):
                ring = at < 0 or at >= rows
                part = slice(RING + at, RING + at + chunk)
                if ring and sizes == GROUPS[0]:
                    sums = [[None, None], [None, None]]
                else:
                    sums = [[acc[ti, f, h, part, :] for h in range(2)] for f in range(2)]
                middle = [cen[ti, h, part, :] for h in range(2)]
                for size in sizes:
                    for s in ((-size, size) if size else (0,)):
                        low, high = inner_rows(s)
                        if not low <= at < high:
                            view_step(view_of(ti, s), s, at, middle, sums)
                for f in range(2):
                    for h in range(2):
                        acc[ti, f, h, part, :] = sums[f][h]
        for size in sizes:
            if size == 0:
                packed_rows(HALF, 0, PAD)
                packed_rows(HALF, PAD + rows, full)
            else:
                packed_rows(HALF - size, 0, PAD)
                packed_rows(HALF + size, PAD + rows, full)
            for s in ((-size, size) if size else (0,)):
                low, high = inner_rows(s)
                packed_step(HALF + s, -RING, low)
                packed_step(HALF + s, high, rows + RING)

    combine(PAD, rows - PAD)
    for sizes in GROUPS:
        for size in sizes:
            if size:
                arrive(row_copies[2 * size : 2 * size + 2])
        edge_sizes(sizes)
    combine(-RING, PAD)
    combine(rows - PAD, rows + RING)

    inside = (gcol >= 0) & (gcol < ncol * cols) & (grow >= 0) & (grow < nrow * rows)
    coeff = damping + own[0] * (0.25 / VIEWS)
    field = own[1] * (-0.5 / VIEWS)
    diag = jnp.where(inside, coeff + weights, 1.0)
    zf = jnp.where(inside, field / diag, 0.0)
    inner = (slice(RING, RING + rows), slice(LANES, LANES + cols))
    source, zed = field[inner], zf[inner]

    def gather(z):
        return edge_e * east(z) + edge_w * west(z) + edge_s * south(z) + edge_n * north(z)

    around = gather(zf)
    yf = around / diag
    n1, y = around[inner], yf[inner]
    n2 = gather(yf)[inner]
    w = source - n1
    q = zed - y
    wv = n1 - n2
    v = w - wv
    sums = (y * n1, q * n1, q * w, y * wv, y * v, q * v)
    line = lax.broadcasted_iota(jnp.int32, (1, LANES), 1)
    packed = jnp.zeros((1, LANES), F32)
    for i, x in enumerate(sums):
        x = jnp.sum(x, axis=0, keepdims=True)
        x = jnp.sum(x, axis=1, keepdims=True)
        packed = jnp.where(line == i, x, packed)
    for step in range(6, len(rounds) + 1):
        learn(step)
    redout[0] = packed
    redbuf[me] = packed

    def red_copy(i):
        peer = (me + i) % count
        return pltpu.make_async_remote_copy(
            src_ref=redout.at[0], dst_ref=redbuf.at[me], send_sem=rsend.at[0], recv_sem=rrecv.at[0],
            device_id=(peer // ncol, peer % ncol), device_id_type=pl.DeviceIdType.MESH)

    def cast_out(i, carry):
        red_copy(i).start()
        return carry

    lax.fori_loop(1, count, cast_out, 0)
    drain(row_copies + side_copies + col_copies)
    others = redbuf.at[pl.ds(0, count - 1)]
    pltpu.make_async_copy(others, others, rrecv.at[0]).wait()
    pltpu.make_async_copy(others, others, rsend.at[0]).wait()
    totals = jnp.sum(redbuf[...], axis=0)
    f, g, h, k, l, m = [totals[:, i : i + 1] for i in range(6)]
    b, e = g + h, f + g
    delta = e / b
    step0 = (e + b) / b
    rz0 = e + b
    rz1 = f - 2.0 * delta * g + delta * delta * h
    wu1 = k - 2.0 * delta * l + delta * delta * m
    beta = rz1 / rz0
    step1 = rz1 / (wu1 - beta * rz1 / step0)
    direction = (y - delta * q) + beta * zed
    image = (wv - delta * v) + beta * w
    out[0] = step0 * zed + step1 * direction
    out[1] = (n1 - delta * w) - step1 * image


def solution(mesh):
    nrow, ncol = mesh.shape["row"], mesh.shape["col"]

    def shards(views):
        _, rows, cols = views.shape
        full = PAD + rows + PAD
        bf = views.dtype
        out = pl.pallas_call(
            functools.partial(kernel, nrow, ncol),
            out_shape=jax.ShapeDtypeStruct((2, rows, cols), F32),
            in_specs=[pl.BlockSpec(memory_space=pltpu.HBM)],
            out_specs=pl.BlockSpec(memory_space=pltpu.VMEM),
            scratch_shapes=[
                pltpu.VMEM((VIEWS, full, cols), bf),
                pltpu.VMEM((2, 5, rows, LANES), bf),
                pltpu.VMEM((5, full, LANES), bf),
                pltpu.VMEM((5, full, LANES), bf),
                pltpu.VMEM((full, LANES), bf),
                pltpu.VMEM((full, LANES), bf),
                pltpu.VMEM((VIEWS, 2, full + 2 * RING, LANES), F32),
                pltpu.VMEM((VIEWS, 2, full + 2 * RING, LANES), F32),
                pltpu.VMEM((ANG, cols, cols), bf),
                pltpu.VMEM((ANG, full + 2 * RING, LANES), F32),
                pltpu.VMEM((ANG, 2, rows + 2 * RING, LANES), F32),
                pltpu.VMEM((rows + 2 * RING, LANES), F32),
                pltpu.VMEM((ANG, 2, 2, rows + 2 * RING, LANES), F32),
                pltpu.VMEM((2, rows + 2 * RING, LANES), F32),
                pltpu.VMEM((2, rows + 2 * RING, cols + 2 * LANES), F32),
                pltpu.VMEM((nrow * ncol, 1, LANES), F32),
                pltpu.VMEM((1, 1, LANES), F32),
                pltpu.SemaphoreType.DMA((ANG,)),
                pltpu.SemaphoreType.DMA((22,)),
                pltpu.SemaphoreType.DMA((22,)),
                pltpu.SemaphoreType.DMA((1,)),
                pltpu.SemaphoreType.DMA((1,)),
                pltpu.SemaphoreType.REGULAR((8,)),
            ],
            compiler_params=pltpu.CompilerParams(collective_id=0, has_side_effects=True, vmem_limit_bytes=48 << 20),
        )(pltpu.with_memory_space_constraint(views, pltpu.HBM))
        return out[0], out[1]

    return jax.shard_map(
        shards,
        mesh=mesh,
        in_specs=(P(None, "row", "col"),),
        out_specs=(P("row", "col"), P("row", "col")),
        check_vma=False,
    )
```

time: 23.3 us -> 21.7 us (0.931)
  Pallas kernels: 21.9 us -> 20.2 us
    pallas_call x1, Pallas kernels: 21.9 us -> 20.2 us  [shards(): pl.pallas_call(functools.partial(kernel, nrow, ncol), out_shape=jax.Shape...]
where the time goes in v2:
time: 21.7 us; the launch traced here: 21.5 us
  Pallas kernels  20.2 us (93%)
  local copies, waits for them, and re-layouts  0.66 us (3%)
  between operations  0.64 us (3%)
    pallas_call x1, Pallas kernels, shards(): pl.pallas_call(functools.partial(kernel, nrow, ncol), out_shape=jax.Shape...  20.2 us
    squeeze x1, local copies, waits for them, and re-layouts, shards(): return (out[0], out[1])  0.66 us

profile of v2, /device:TPU:0, one launch (start us, length us, event | category | flops | bytes accessed | tf_op | source)
XLA Modules:
  0.0 21.5 jit_solution(15888030850588911958)
XLA Ops:
  0.6 20.2 %shard_map.30 = f32[2,64,256]{2,1,0:T(8,128)S(1)} custom-call(bf16[81,64,256]{2,1,0:T(8,128)(2,1)} %views.1), custom_call_target="tpu_custom_call" | custom-call | tf_op jit(solution)/shard_map/pallas_call | solution.py:500
  20.8 0.7 %slice_bitcast_fusion = (f32[64,256]{1,0:T(8,128)}, f32[64,256]{1,0:T(8,128)}) fusion(f32[2,64,256]{2,1,0:T(8,128)S(1)} %shard_map.30), kind=kLoop, calls=%fused_computation | loop fusion | bytes 262144 | tf_op jit(solution)/shard_map/squeeze | solution.py:532

commit v3 on v2

--- a/solution.py
+++ b/solution.py
@@ -59,9 +59,14 @@
         pl.semaphore_wait(sem, total)
 
     greet(barrier, 1, DIRS[:4])
-    rounds = [(1, DIRS[:4])]
-    while len(rounds) == 1 or 2 * rounds[-1][0] < max(nrow, ncol) - 1:
-        rounds.append((1 << (len(rounds) - 1), DIRS))
+    rounds = []
+    while 1 << len(rounds) < nrow + ncol - 2:
+        half = (1 << len(rounds)) // 2
+        if half:
+            steps = [(i, j) for i in range(-2, 3) for j in range(-2, 3) if 0 < abs(i) + abs(j) <= 2]
+            rounds.append((half, steps))
+        else:
+            rounds.append((1, DIRS[:4]))
 
     def learn(step):
         if 0 < step <= len(rounds):
@@ -169,29 +174,32 @@
     start(row_copies)
     start(side_copies[:2])
     learn(0)
-    for copy in loads:
-        copy.wait()
 
     lane = lane_of(rows)
-    right_part = lane < 64
 
     def own_start(t):
         return STRIP[t] + (2 if t else 1)
 
+    def narrow_lane(size):
+        return lane_of(size).astype(F32).astype(sp.dtype)
+
+    nlane = narrow_lane(rows)
     for slot, pair in enumerate(((0, 1), (2, 3), (4,), (5, 6), (7, 8))):
         left = right = None
+        for si in pair:
+            loads[si].wait()
         for half, si in enumerate(pair):
             for t in range(HALF, -1, -1):
                 first = own_start(t) + 64 * half
-                x = roll(ext[si * ANG + HALF + t, PAD : PAD + rows, 0:LANES].astype(F32), first)
-                left = x if left is None else jnp.where(lane >= first, x, left)
+                x = roll(ext[si * ANG + HALF + t, PAD : PAD + rows, 0:LANES], first)
+                left = x if left is None else jnp.where(nlane >= first, x, left)
         for half, si in reversed(list(enumerate(pair))):
             for t in range(HALF, -1, -1):
                 first = STRIP[t] + 64 * (1 - half)
-                x = roll(ext[si * ANG + HALF - t, PAD : PAD + rows, cols - LANES : cols].astype(F32), first - (LANES - 3 - D0 * t))
-                right = x if right is None else jnp.where(lane >= first, x, right)
-        sp[0, slot] = left.astype(sp.dtype)
-        sp[1, slot] = right.astype(sp.dtype)
+                x = roll(ext[si * ANG + HALF - t, PAD : PAD + rows, cols - LANES : cols], first - (LANES - 3 - D0 * t))
+                right = x if right is None else jnp.where(nlane >= first, x, right)
+        sp[0, slot] = left
+        sp[1, slot] = right
     start(col_copies[:2])
     learn(1)
     start(side_copies[2:] + col_copies[2:])
@@ -199,34 +207,32 @@
 
     def build_center(low, high):
         part, into = slice(PAD + low, PAD + high), slice(RING + low, RING + high)
-        at = lane_of(high - low)
-        tl, tr = side_l[part, :].astype(F32), side_r[part, :].astype(F32)
-        ta, tb = [ext[CENTER, part, h * LANES : (h + 1) * LANES].astype(F32) for h in range(2)]
+        at = narrow_lane(high - low)
+        tl, tr = side_l[part, :], side_r[part, :]
+        ta, tb = [ext[CENTER, part, h * LANES : (h + 1) * LANES] for h in range(2)]
         for ti in range(ANG):
             move = D0 * (ti - HALF)
             if move > 0:
                 ra = roll(ta, move)
-                cen[ti, 0, into, :] = jnp.where(at >= move, ra, roll(tl, move))
-                cen[ti, 1, into, :] = jnp.where(at >= move, roll(tb, move), ra)
+                pair = jnp.where(at >= move, ra, roll(tl, move)), jnp.where(at >= move, roll(tb, move), ra)
             elif move < 0:
                 rb = roll(tb, move)
-                cen[ti, 0, into, :] = jnp.where(at < LANES + move, roll(ta, move), rb)
-                cen[ti, 1, into, :] = jnp.where(at < LANES + move, rb, roll(tr, move))
+                pair = jnp.where(at < LANES + move, roll(ta, move), rb), jnp.where(at < LANES + move, rb, roll(tr, move))
             else:
-                cen[ti, 0, into, :] = ta
-                cen[ti, 1, into, :] = tb
+                pair = ta, tb
+            for h in range(2):
+                cen[ti, h, into, :] = pair[h].astype(F32)
         total = None
         for t in range(HALF, -1, -1):
-            m = D0 * t
             first = STRIP[t]
-            inside = own_start(t) + m
+            inside = own_start(t) + D0 * t
             x = jnp.where(at >= inside, roll(tr, inside), roll(tb, inside))
             total = x if total is None else jnp.where(at >= first, x, total)
         for t in range(HALF, -1, -1):
             first = 64 + STRIP[t]
             x = jnp.where(at >= first + 3, roll(ta, first + 3), roll(tl, first + 3))
             total = jnp.where(at >= first, x, total)
-        cpack[into, :] = total
+        cpack[into, :] = total.astype(F32)
 
     build_center(0, rows)
     pacc[...] = jnp.zeros_like(pacc)
@@ -289,7 +295,7 @@
 
     for ti in range(ANG):
         inner_pass(ti)
-        if ti % 3 == 2:
+        if ti in (2, 5):
             learn(ti // 3 + 2)
     arrive(row_copies[:2] + col_copies + side_copies[2:])
     build_center(-RING, 0)
@@ -322,20 +328,20 @@
 
     def packed_rows(si, low, high):
         slot, half = ((0, 0), (0, 1), (1, 0), (1, 1), (2, 0), (3, 0), (3, 1), (4, 0), (4, 1))[si]
-        at = lane_of(high - low)
+        at = narrow_lane(high - low)
         part = slice(low, high)
-        x, z = col_r[slot, part, :].astype(F32), col_l[slot, part, :].astype(F32)
+        x, z = col_r[slot, part, :], col_l[slot, part, :]
         merged = roll(jnp.where(at < 64, z, x), 64) if half else jnp.where(at < 64, x, z)
         for t in range(HALF + 1):
-            a = ext[si * ANG + HALF - t, part, 0:LANES].astype(F32)
-            b = ext[si * ANG + HALF + t, part, cols - LANES : cols].astype(F32)
+            a = ext[si * ANG + HALF - t, part, 0:LANES]
+            b = ext[si * ANG + HALF + t, part, cols - LANES : cols]
             first, last = STRIP[t], own_start(t) - 1
             own_b = (at >= first) & (at <= last) if t else at == first
             merged = jnp.where(own_b, roll(b, last - (LANES - 1)), merged)
             first = 64 + STRIP[t] + 3 + D0 * t
-            own_a = (at == first) | (at == first + 1) if t else at == first
+            own_a = (at >= first) & (at <= first + 1) if t else at == first
             merged = jnp.where(own_a, roll(a, first), merged)
-        pb[si, RING + low : RING + high, :] = merged
+        pb[si, RING + low : RING + high, :] = merged.astype(F32)
 
     def packed_step(si, low, high):
         s = si - HALF
@@ -356,7 +362,7 @@
     for si in range(ANG):
         packed_rows(si, PAD, PAD + rows)
         packed_step(si, *inner_rows(si - HALF))
-    learn(5)
+    learn(4)
 
     def combine(low, high):
         part = slice(RING + low, RING + high)
@@ -454,7 +460,7 @@
         x = jnp.sum(x, axis=0, keepdims=True)
         x = jnp.sum(x, axis=1, keepdims=True)
         packed = jnp.where(line == i, x, packed)
-    for step in range(6, len(rounds) + 1):
+    for step in range(5, len(rounds) + 1):
         learn(step)
     redout[0] = packed
     redbuf[me] = packed

time: 21.7 us -> 21.6 us (level)
  no operation moved by 1% of the time
where the time goes in v3:
time: 21.6 us; the launch traced here: 21.4 us
  Pallas kernels  20.1 us (93%)
  local copies, waits for them, and re-layouts  0.66 us (3%)
  between operations  0.64 us (3%)
    pallas_call x1, Pallas kernels, shards(): pl.pallas_call(functools.partial(kernel, nrow, ncol), out_shape=jax.Shape...  20.1 us
    squeeze x1, local copies, waits for them, and re-layouts, shards(): return (out[0], out[1])  0.66 us

profile of v3, /device:TPU:0, one launch (start us, length us, event | category | flops | bytes accessed | tf_op | source)
XLA Modules:
  0.0 21.4 jit_solution(7434204197124773939)
XLA Ops:
  0.6 20.1 %shard_map.30 = f32[2,64,256]{2,1,0:T(8,128)S(1)} custom-call(bf16[81,64,256]{2,1,0:T(8,128)(2,1)} %views.1), custom_call_target="tpu_custom_call" | custom-call | tf_op jit(solution)/shard_map/pallas_call | solution.py:506
  20.8 0.7 %slice_bitcast_fusion = (f32[64,256]{1,0:T(8,128)}, f32[64,256]{1,0:T(8,128)}) fusion(f32[2,64,256]{2,1,0:T(8,128)S(1)} %shard_map.30), kind=kLoop, calls=%fused_computation | loop fusion | bytes 262144 | tf_op jit(solution)/shard_map/squeeze | solution.py:538
